TPU v7x, 256 devices: a whole 4x4x8 slice. The times are simulated.
256 devices in a mesh: ctx: 32 (over z, x), head: 8 (over y, core).
Axes of the slice: x: 4, y: 4, z: 8, core: 2. Of those that a mesh axis runs over, the one named last changes fastest.
Arguments:
- query_rows: bfloat16 [98304, 4096], P('ctx', 'head'), may hold values from -6 to 6
- key_rows: bfloat16 [98304, 4096], P('ctx', 'head'), may hold values from -6 to 6
- value_rows: bfloat16 [98304, 4096], P('ctx', 'head'), may hold values from -220 to 220
- out_gain: bfloat16 [4096], P('head'), may hold values from 0.5 to 1.5
- doc_starts: int32 [16], replicated, may hold values from 0 to 98303, as said below
Outputs:
- normed: bfloat16 [98304, 4096], P('ctx', 'head')
Inputs may be any that keep to these rules, and one draw needn't show every extreme that they name: `doc_starts`: ascending and distinct, the first entry 0, the last entry 98303.
All inputs are finite; a program needn't handle non-finite values.
Results may differ from a plain program's by a relative error of at most 0.001.
Values sent between devices are 32-bit elements; how exact they have to be, the bound alone decides.
A program may use at most 128 MiB of HBM per device.

v0:
```python
import jax
import jax.numpy as jnp
from jax import lax
from jax.sharding import PartitionSpec as P

HEADS = 32
HD = 128
BLOCK = 512


def entering(shard, axis, combine, identity):
    peers, mine = (lax.axis_size(axis), lax.axis_index(axis))
    everything = jax.tree.map(lambda part: lax.all_gather(part, axis), shard)
    start = jax.tree.map(
        lambda part, zero: jnp.broadcast_to(jnp.asarray(zero, part.dtype), part.shape),
        shard,
        identity,
    )

    def hop(k, before):
        reached = k < mine
        new = combine(before, jax.tree.map(lambda part: part[k], everything))
        return jax.tree.map(lambda a, b: jnp.where(reached, a, b), new, before)

    return lax.fori_loop(0, peers, hop, start)


def segment_of(positions, doc_starts):
    return jnp.sum((doc_starts <= positions[..., None]).astype(jnp.int32), axis=-1) - 1


def shards(query_rows, key_rows, value_rows, out_gain, doc_starts):
    row_count, feature_count = query_rows.shape
    head_count = feature_count // HD
    block_count = row_count // BLOCK
    device = lax.axis_index("ctx")
    anchor = device * row_count
    queries = query_rows.reshape(block_count, BLOCK, head_count, HD)
    keyset = key_rows.reshape(block_count, BLOCK, head_count, HD)
    valueset = value_rows.reshape(block_count, BLOCK, head_count, HD)
    positions = anchor + jnp.arange(row_count, dtype=jnp.int32).reshape(block_count, BLOCK)
    segment = segment_of(positions, doc_starts)
    before = segment_of(positions[:, 0] - 1, doc_starts)
    tail_mask = (segment == segment[:, -1:])[:, :, None, None]
    masked_keys = jnp.where(tail_mask, keyset, jnp.zeros((), jnp.bfloat16))
    contrib = jnp.einsum(
        "bihd,bihe->bhde", masked_keys, valueset, preferred_element_type=jnp.float32
    )
    block_flags = segment[:, -1] != before
    empty = jnp.zeros((head_count, HD, HD), jnp.float32)
    summary = empty
    for number in range(block_count):
        summary = jnp.where(block_flags[number], contrib[number], summary + contrib[number])
    highest = lax.Precision.HIGHEST
    device_flag = jnp.max(block_flags.astype(jnp.float32)).reshape(1)

    def combine(earlier, later):
        joined = jnp.where(later[1][0] > 0.0, later[0], earlier[0] + later[0])
        return (joined, jnp.maximum(earlier[1], later[1]))

    incoming, _ = entering(
        (summary, device_flag), "ctx", combine, (empty, jnp.zeros((1,), jnp.float32))
    )
    causal = jnp.arange(BLOCK)[:, None] >= jnp.arange(BLOCK)[None, :]
    carried = incoming
    results = []
    for number in range(block_count):
        seg_blk = segment[number]
        scores = jnp.einsum(
            "ihd,jhd->hij", queries[number], keyset[number], preferred_element_type=jnp.float32
        )
        allowed = causal & (seg_blk[:, None] == seg_blk[None, :])
        scores = jnp.where(allowed[None], scores, jnp.float32(0.0))
        within = jnp.einsum(
            "hij,jhe->ihe", scores, valueset[number].astype(jnp.float32), precision=highest
        )
        across = jnp.einsum(
            "ihd,hde->ihe", queries[number].astype(jnp.float32), carried, precision=highest
        )
        live = (seg_blk == before[number])[:, None, None]
        results.append(within + jnp.where(live, across, jnp.float32(0.0)))
        carried = jnp.where(block_flags[number], contrib[number], carried + contrib[number])
    attended = jnp.concatenate(results, axis=0).reshape(row_count, feature_count)
    local_squares = jnp.sum(attended * attended, axis=1)
    totals = lax.psum(local_squares, "head")
    normed = (
        attended
        * lax.rsqrt(totals[:, None] / (HEADS * HD) + 1e-06)
        * out_gain.astype(jnp.float32)[None, :]
    )
    return normed.astype(jnp.bfloat16)


def solution(mesh):
    placed = (P("ctx", "head"), P("ctx", "head"), P("ctx", "head"), P("head"), P())
    return jax.shard_map(
        shards, mesh=mesh, in_specs=placed, out_specs=P("ctx", "head"), check_vma=False
    )
```

profile of v0, /device:TPU:1, one launch (start us, length us, event | category | flops | bytes accessed | tf_op | source)
XLA Modules:
  0.0 316.1 jit_solution(11716001103655603164)
XLA Ops:
  9.9 5.5 %reshape.367 = bf16[6,512,4,128]{3,2,1,0:T(4,128)(2,1)} reshape(bf16[3072,512]{1,0:T(8,128)(2,1)} %param.8) | data formatting | bytes 6291456 | tf_op jit(solution)/shard_map/reshape | solution.py:39
  15.3 6.1 %copy.351 = bf16[6,512,4,128]{1,3,2,0:T(8,128)(2,1)} copy(bf16[6,512,4,128]{3,2,1,0:T(4,128)(2,1)} %reshape.367) | data formatting | bytes 6291456 | tf_op jit(solution)/shard_map/reshape | solution.py:39
  21.4 2.9 reshape.368
  24.3 3.8 %fusion.15 = f32[6,4,128,128]{3,2,1,0:T(8,128)S(1)} fusion(bf16[6,512,4,128]{3,2,1,0:T(4,128)(2,1)} %reshape.368, bf16[6,512,4,128]{1,3,2,0:T(8,128)(2,1)} %copy.351, pred[6,512]{1,0:T(8,128)(4,1)S(1)} %broadcast_compare_fusion), kind=kOutput, calls=%fused_computation.19 | convolution fusion | flops 404226048 | bytes 7867392 | tf_op jit(solution)/shard_map/bihd,bihe->bhde/dot_general | solution.py:46
  29.3 4.1 %add_select_fusion.6 = f32[1,4,128,128]{3,2,1,0:T(8,128)} fusion(f32[6,4,128,128]{3,2,1,0:T(8,128)S(1)} %fusion.15, pred[]{:T(512)} %bitcast.13, pred[]{:T(512)} %bitcast.12, pred[]{:T(512)} %bitcast.11, pred[]{:T(512)} %bitcast.10, pred[]{:T(512)} %bitcast.9), kind=kLoop, calls=%fused_computation.78 | loop fusion | flops 655360 | bytes 1835013 | tf_op jit(solution)/shard_map/jit(_where)/select_n | solution.py:53
  33.4 3.7 %fusion.89 = (bf16[512,512]{1,0:T(8,128)(2,1)}, bf16[512,512]{1,0:T(8,128)(2,1)}, bf16[512,512]{1,0:T(8,128)(2,1)}, bf16[512,512]{1,0:T(8,128)(2,1)}, bf16[512,512]{1,0:T(8,128)(2,1)}, /*index=5*/bf16[512,512]{1,0:T(8,128)(2,1)}) fusion(bf16[3072,512]{1,0:T(8,128)(2,1)} %param.7), kind=kLoop, calls=%fused_computation.113 | loop fusion | bytes 6291456 | tf_op jit(solution)/shard_map/slice | solution.py:70
  37.1 2.0 copy.439
  40.8 2.1 copy.440
  42.9 3.5 %fusion.90 = (bf16[512,512]{1,0:T(8,128)(2,1)}, bf16[512,512]{1,0:T(8,128)(2,1)}, bf16[512,512]{1,0:T(8,128)(2,1)}, bf16[512,512]{1,0:T(8,128)(2,1)}, bf16[512,512]{1,0:T(8,128)(2,1)}, /*index=5*/bf16[512,512]{1,0:T(8,128)(2,1)S(1)}) fusion(bf16[3072,512]{1,0:T(8,128)(2,1)} %param.9), kind=kLoop, calls=%fused_computation.114 | loop fusion | bytes 6291456 | tf_op jit(solution)/shard_map/slice | solution.py:75
  48.7 2.1 copy.444
  52.0 2.1 copy.447
  54.4 2.3 copy.449
  57.9 2.1 copy.452
  60.0 2.1 copy.453
  63.3 2.1 copy.455
  65.4 2.1 copy.456
  69.3 66.2 %all-reduce = f32[32]{0:T(128)S(1)} all-reduce(f32[32]{0:T(128)S(1)} %dynamic-update-slice), channel_id=1, replica_groups=mesh['ctx'=32,'head'=8] {'ctx'}, use_global_device_ids=true, to_apply=%add | all-reduce | flops 32 | bytes 256
  141.3 1.8 fusion.94
  147.1 3.2 %fusion.50 = f32[512,4,128]{2,0,1:T(8,128)} fusion(bf16[512,4,128]{0,2,1:T(8,128)(2,1)S(1)} %bitcast.160, f32[4,512,512]{2,1,0:T(8,128)S(1)} %fusion.94, pred[512,512]{1,0:T(8,128)(4,1)S(1)} %fusion.73), kind=kOutput, calls=%fused_computation.60 | convolution fusion | flops 1611661312 | bytes 6029312 | tf_op jit(solution)/shard_map/hij,jhe->ihe/dot_general | solution.py:74
  150.3 3.2 %fusion.53 = f32[512,4,128]{2,0,1:T(8,128)} fusion(bf16[512,4,128]{0,2,1:T(8,128)(2,1)S(1)} %bitcast.161, f32[4,512,512]{2,1,0:T(8,128)S(1)} %fusion.95, pred[512,512]{1,0:T(8,128)(4,1)S(1)} %fusion.72), kind=kOutput, calls=%fused_computation.61 | convolution fusion | flops 1611661312 | bytes 6029312 | tf_op jit(solution)/shard_map/hij,jhe->ihe/dot_general | solution.py:74
  153.6 3.5 %fusion.56 = f32[512,4,128]{2,0,1:T(8,128)} fusion(bf16[512,4,128]{0,2,1:T(8,128)(2,1)S(1)} %bitcast.163, f32[4,512,512]{2,1,0:T(8,128)S(1)} %fusion.96, pred[512,512]{1,0:T(8,128)(4,1)S(1)} %fusion.71), kind=kOutput, calls=%fused_computation.62 | convolution fusion | flops 1611661312 | bytes 6029312 | tf_op jit(solution)/shard_map/hij,jhe->ihe/dot_general | solution.py:74
  157.0 3.3 %fusion.59 = f32[512,4,128]{2,0,1:T(8,128)} fusion(bf16[512,4,128]{0,2,1:T(8,128)(2,1)S(1)} %bitcast.164, f32[4,512,512]{2,1,0:T(8,128)S(1)} %fusion.97, pred[512,512]{1,0:T(8,128)(4,1)S(1)} %fusion.70), kind=kOutput, calls=%fused_computation.63 | convolution fusion | flops 1611661312 | bytes 6029312 | tf_op jit(solution)/shard_map/hij,jhe->ihe/dot_general | solution.py:74
  160.3 3.2 %fusion.62 = f32[512,4,128]{2,0,1:T(8,128)} fusion(bf16[512,4,128]{0,2,1:T(8,128)(2,1)S(1)} %bitcast.165, f32[4,512,512]{2,1,0:T(8,128)S(1)} %fusion.98, pred[512,512]{1,0:T(8,128)(4,1)S(1)} %fusion.69), kind=kOutput, calls=%fused_computation.64 | convolution fusion | flops 1611661312 | bytes 6029312 | tf_op jit(solution)/shard_map/hij,jhe->ihe/dot_general | solution.py:74
  163.6 3.2 %fusion.65 = f32[512,4,128]{2,0,1:T(8,128)} fusion(bf16[512,4,128]{0,2,1:T(8,128)(2,1)S(1)} %bitcast.166, f32[4,512,512]{2,1,0:T(8,128)S(1)} %fusion.99, pred[512,512]{1,0:T(8,128)(4,1)S(1)} %fusion.68), kind=kOutput, calls=%fused_computation.65 | convolution fusion | flops 1611661312 | bytes 6029312 | tf_op jit(solution)/shard_map/hij,jhe->ihe/dot_general | solution.py:74
  166.8 74.9 %while.14 = (s32[]{:T(128)}, f32[4,128,128]{2,1,0:T(8,128)S(1)}, s32[]{:T(128)}, f32[32,1]{0,1:T(1,128)S(1)}, f32[32,4,128,128]{3,2,1,0:T(8,128)}, /*index=5*/s32[]{:T(128)}, s32[]{:T(128)}) while((s32[]{:T(128)}, f32[4,128,128]{2,1,0:T(8,128)S(1)}, s32[]{:T(128)}, f32[32,1]{0,1:T(1,128)S(1)}, f32[32,4,128,128]{3,2,1,0:T(8,128)}, ...), condition=%wide.region_4.5_spmd.clone, body=%wide.region_3.4_spmd.clone.sunk | while | flops 262149 | bytes 786543 | solution.py:25
  167.4 1.7 fusion.130
  169.8 1.7 fusion.130
  172.1 1.7 fusion.130
  174.4 1.7 fusion.130
  176.8 1.7 fusion.130
  179.1 1.7 fusion.130
  181.5 1.7 fusion.130
  183.8 1.7 fusion.130
  186.1 1.7 fusion.130
  188.5 1.7 fusion.130
  190.8 1.7 fusion.130
  193.2 1.7 fusion.130
  195.5 1.7 fusion.130
  197.8 1.7 fusion.130
  200.2 1.7 fusion.130
  202.5 1.7 fusion.130
  204.9 1.7 fusion.130
  207.2 1.7 fusion.130
  209.5 1.7 fusion.130
  211.9 1.7 fusion.130
  214.2 1.7 fusion.130
  216.6 1.7 fusion.130
  218.9 1.7 fusion.130
  221.2 1.7 fusion.130
  223.6 1.7 fusion.130
  225.9 1.7 fusion.130
  228.3 1.7 fusion.130
  230.6 1.7 fusion.130
  232.9 1.7 fusion.130
  241.7 2.9 add_select_fusion.2
  244.7 3.0 fusion.34
  247.7 2.3 fusion.37
  251.6 2.3 fusion.43
  255.6 2.3 fusion.49
  257.9 6.6 %copy.401 = f32[3072,4,128]{0,2,1:T(8,128)} copy(f32[3072,4,128]{2,0,1:T(8,128)} %fusion.49) | data formatting | bytes 12582912 | tf_op jit(solution)/shard_map/concatenate | solution.py:83
  264.4 3.3 %multiply_reduce_fusion = f32[3072]{0:T(1024)S(1)} fusion(f32[3072,4,128]{2,0,1:T(8,128)} %fusion.49), kind=kLoop, calls=%fused_computation.6 | loop fusion | flops 3142656 | bytes 6303744 | tf_op jit(solution)/shard_map/reduce_sum | solution.py:84
  267.7 35.0 %psum.7 = f32[3072]{0:T(1024)S(1)} all-reduce(f32[3072]{0:T(1024)S(1)} %multiply_reduce_fusion), channel_id=1, replica_groups=mesh['ctx'=32,'head'=8] {'head'}, use_global_device_ids=true, to_apply=%region_6.7 | all-reduce | flops 3072 | bytes 24576 | tf_op jit(solution)/shard_map/psum | solution.py:85
  302.7 3.8 %fusion.2 = bf16[3072,512]{0,1:T(8,128)(2,1)S(1)} fusion(f32[3072,4,128]{0,2,1:T(8,128)} %copy.401, f32[512]{0:T(512)S(1)} %convert_element_type.13, f32[3072]{0:T(1024)S(1)} %add_rsqrt_fusion), kind=kLoop, calls=%fused_computation.5 | loop fusion | flops 4718592 | bytes 9451520 | tf_op jit(solution)/shard_map/convert_element_type | solution.py:91
  306.5 2.8 copy.402
  (157 shorter events, 51.9 us)
Async XLA Ops:
  6.5 160.3 %all-gather.2.cloned.1.call-start = ((), (), s32[]{:S(2)}) async-start(), calls=%async_computation | async-start | bytes 8650752 | tf_op jit(solution)/shard_map/all_gather | solution.py:13
  15.3 6.1 %copy-start.1 = (bf16[3072,512]{1,0:T(8,128)(2,1)S(1)}, bf16[3072,512]{1,0:T(8,128)(2,1)}, u32[]{:S(2)}) copy-start(bf16[3072,512]{1,0:T(8,128)(2,1)} %param.9) | copy-start | bytes 9437188
  28.2 1.1 copy-start.2
  33.4 5.8 %copy-start = (bf16[3072,512]{1,0:T(8,128)(2,1)S(1)}, bf16[3072,512]{1,0:T(8,128)(2,1)}, u32[]{:S(2)}) copy-start(bf16[3072,512]{1,0:T(8,128)(2,1)} %param.8) | copy-start | bytes 9437188
  40.8 6.6 %copy-start.30 = (bf16[512,512]{1,0:T(8,128)(2,1)S(1)}, bf16[512,512]{1,0:T(8,128)(2,1)}, u32[]{:S(2)}) copy-start(bf16[512,512]{1,0:T(8,128)(2,1)} %get-tuple-element.142) | copy-start | bytes 1572868
  42.9 4.7 %copy-start.33 = (bf16[512,512]{1,0:T(8,128)(2,1)S(1)}, bf16[512,512]{1,0:T(8,128)(2,1)}, u32[]{:S(2)}) copy-start(bf16[512,512]{1,0:T(8,128)(2,1)} %get-tuple-element.136) | copy-start | bytes 1572868
  42.9 7.9 %copy-start.29 = (bf16[512,512]{1,0:T(8,128)(2,1)S(1)}, bf16[512,512]{1,0:T(8,128)(2,1)}, u32[]{:S(2)}) copy-start(bf16[512,512]{1,0:T(8,128)(2,1)} %get-tuple-element.141) | copy-start | bytes 1572868
  46.4 4.6 %copy-start.31 = (bf16[512,512]{1,0:T(8,128)(2,1)S(1)}, bf16[512,512]{1,0:T(8,128)(2,1)}, u32[]{:S(2)}) copy-start(bf16[512,512]{1,0:T(8,128)(2,1)} %get-tuple-element.135) | copy-start | bytes 1572868
  46.4 7.7 %copy-start.28 = (bf16[512,512]{1,0:T(8,128)(2,1)S(1)}, bf16[512,512]{1,0:T(8,128)(2,1)}, u32[]{:S(2)}) copy-start(bf16[512,512]{1,0:T(8,128)(2,1)} %get-tuple-element.140) | copy-start | bytes 1572868
  47.7 95.5 %copy-start.5 = (bf16[512,512]{0,1:T(8,128)(2,1)}, bf16[512,512]{0,1:T(8,128)(2,1)S(1)}, u32[]{:S(2)}) copy-start(bf16[512,512]{0,1:T(8,128)(2,1)S(1)} %copy.442) | copy-start | bytes 1572868
  47.7 10.0 %copy-start.27 = (bf16[512,512]{1,0:T(8,128)(2,1)S(1)}, bf16[512,512]{1,0:T(8,128)(2,1)}, u32[]{:S(2)}) copy-start(bf16[512,512]{1,0:T(8,128)(2,1)} %get-tuple-element.139) | copy-start | bytes 1572868
  51.0 93.0 %copy-start.7 = (bf16[512,512]{0,1:T(8,128)(2,1)}, bf16[512,512]{0,1:T(8,128)(2,1)S(1)}, u32[]{:S(2)}) copy-start(bf16[512,512]{0,1:T(8,128)(2,1)S(1)} %copy.445) | copy-start | bytes 1572868
  51.0 5.7 %copy-start.32 = (bf16[512,512]{1,0:T(8,128)(2,1)S(1)}, bf16[512,512]{1,0:T(8,128)(2,1)}, u32[]{:S(2)}) copy-start(bf16[512,512]{1,0:T(8,128)(2,1)} %get-tuple-element.146) | copy-start | bytes 1572868
  54.4 90.4 %copy-start.9 = (bf16[512,512]{0,1:T(8,128)(2,1)}, bf16[512,512]{0,1:T(8,128)(2,1)S(1)}, u32[]{:S(2)}) copy-start(bf16[512,512]{0,1:T(8,128)(2,1)S(1)} %copy.448) | copy-start | bytes 1572868
  54.4 13.1 %copy-start.34 = (bf16[512]{0:T(512)(128)(2,1)S(1)}, bf16[512]{0:T(512)(128)(2,1)}, u32[]{:S(2)}) copy-start(bf16[512]{0:T(512)(128)(2,1)} %param.10) | copy-start | bytes 3076
  54.4 13.0 %copy-start.35 = (u32[256]{0:T(256)S(1)}, u32[256]{0:T(256)}, u32[]{:S(2)}) copy-start(u32[256]{0:T(256)} %constant.61) | copy-start | bytes 3076
  57.7 83.6 %copy-start.4 = (bf16[512,512]{0,1:T(8,128)(2,1)S(1)}, bf16[512,512]{0,1:T(8,128)(2,1)}, u32[]{:S(2)}) copy-start(bf16[512,512]{0,1:T(8,128)(2,1)} %copy.439) | copy-start | bytes 1572868
  135.5 7.7 %copy-start.22 = (bf16[512,512]{0,1:T(8,128)(2,1)S(1)}, bf16[512,512]{0,1:T(8,128)(2,1)}, u32[]{:S(2)}) copy-start(bf16[512,512]{0,1:T(8,128)(2,1)} %copy.443) | copy-start | bytes 1572868
  141.3 2.7 copy-start.23
  143.2 1.6 copy-start.24
  144.0 1.6 copy-start.25
  144.8 1.6 copy-start.26
  145.5 1.6 copy-start.16
  147.1 3.2 %copy-start.17 = (bf16[512,512]{0,1:T(8,128)(2,1)S(1)}, bf16[512,512]{0,1:T(8,128)(2,1)}, u32[]{:S(2)}) copy-start(bf16[512,512]{0,1:T(8,128)(2,1)} %copy.444) | copy-start | bytes 1572868
  150.3 3.2 %copy-start.18 = (bf16[512,512]{0,1:T(8,128)(2,1)S(1)}, bf16[512,512]{0,1:T(8,128)(2,1)}, u32[]{:S(2)}) copy-start(bf16[512,512]{0,1:T(8,128)(2,1)} %copy.447) | copy-start | bytes 1572868
  153.6 3.5 %copy-start.19 = (bf16[512,512]{0,1:T(8,128)(2,1)S(1)}, bf16[512,512]{0,1:T(8,128)(2,1)}, u32[]{:S(2)}) copy-start(bf16[512,512]{0,1:T(8,128)(2,1)} %copy.450) | copy-start | bytes 1572868
  157.0 3.3 %copy-start.20 = (bf16[512,512]{0,1:T(8,128)(2,1)S(1)}, bf16[512,512]{0,1:T(8,128)(2,1)}, u32[]{:S(2)}) copy-start(bf16[512,512]{0,1:T(8,128)(2,1)} %copy.453) | copy-start | bytes 1572868
  160.3 3.3 %copy-start.21 = (bf16[512,512]{0,1:T(8,128)(2,1)S(1)}, bf16[512,512]{0,1:T(8,128)(2,1)}, u32[]{:S(2)}) copy-start(bf16[512,512]{0,1:T(8,128)(2,1)} %copy.456) | copy-start | bytes 1572868
  163.6 78.1 %copy-start.3 = (f32[6,4,128,128]{3,2,1,0:T(8,128)S(1)}, f32[6,4,128,128]{3,2,1,0:T(8,128)}, u32[]{:S(2)}) copy-start(f32[6,4,128,128]{3,2,1,0:T(8,128)} %copy-done.2) | copy-start | bytes 4718596
  241.7 6.0 %copy-start.6 = (bf16[512,512]{0,1:T(8,128)(2,1)S(1)}, bf16[512,512]{0,1:T(8,128)(2,1)}, u32[]{:S(2)}) copy-start(bf16[512,512]{0,1:T(8,128)(2,1)} %copy-done.5) | copy-start | bytes 1572868
  241.7 6.0 %copy-start.15 = (f32[512,4,128]{2,0,1:T(8,128)S(1)}, f32[512,4,128]{2,0,1:T(8,128)}, u32[]{:S(2)}) copy-start(f32[512,4,128]{2,0,1:T(8,128)} %fusion.53) | copy-start | bytes 3145732
  241.7 8.2 %copy-start.8 = (bf16[512,512]{0,1:T(8,128)(2,1)S(1)}, bf16[512,512]{0,1:T(8,128)(2,1)}, u32[]{:S(2)}) copy-start(bf16[512,512]{0,1:T(8,128)(2,1)} %copy-done.7) | copy-start | bytes 1572868
  241.7 8.2 %copy-start.12 = (f32[512,4,128]{2,0,1:T(8,128)S(1)}, f32[512,4,128]{2,0,1:T(8,128)}, u32[]{:S(2)}) copy-start(f32[512,4,128]{2,0,1:T(8,128)} %fusion.56) | copy-start | bytes 3145732
  244.6 6.9 %copy-start.10 = (bf16[512,512]{0,1:T(8,128)(2,1)S(1)}, bf16[512,512]{0,1:T(8,128)(2,1)}, u32[]{:S(2)}) copy-start(bf16[512,512]{0,1:T(8,128)(2,1)} %copy-done.9) | copy-start | bytes 1572868
  244.7 6.9 %copy-start.14 = (f32[512,4,128]{2,0,1:T(8,128)S(1)}, f32[512,4,128]{2,0,1:T(8,128)}, u32[]{:S(2)}) copy-start(f32[512,4,128]{2,0,1:T(8,128)} %fusion.59) | copy-start | bytes 3145732
  247.6 6.3 %copy-start.11 = (f32[512,4,128]{2,0,1:T(8,128)S(1)}, f32[512,4,128]{2,0,1:T(8,128)}, u32[]{:S(2)}) copy-start(f32[512,4,128]{2,0,1:T(8,128)} %fusion.62) | copy-start | bytes 3145732
  250.0 5.7 %copy-start.13 = (f32[512,4,128]{2,0,1:T(8,128)S(1)}, f32[512,4,128]{2,0,1:T(8,128)}, u32[]{:S(2)}) copy-start(f32[512,4,128]{2,0,1:T(8,128)} %fusion.65) | copy-start | bytes 3145732
Sparse Core Ops, SparseCore 0:
  33.5 101.7 all-gather.1
where the time goes:
time: 319 us; the launch traced here: 316 us
  blocking collectives  101 us (32%)
  other arithmetic  95.8 us (30%)
  local copies, waits for them, and re-layouts  62.4 us (20%)
  matrix products  42.3 us (13%)
  between operations  13.9 us (4%)
    unnamed x1, blocking collectives  66.2 us
    select_n x32, other arithmetic, hop(): return jax.tree.map(lambda a, b: jnp.where(reached, a, b), new, before)  54.6 us
    psum x1, blocking collectives, shards(): totals = lax.psum(local_squares, 'head')  35 us
    unnamed x93, local copies, waits for them, and re-layouts  28.2 us
    gt x32, other arithmetic, combine(): joined = jnp.where(later[1][0] > 0.0, later[0], earlier[0] + later[0])  19.7 us
    dot_general x6, matrix products, shards(): jnp.einsum('hij,jhe->ihe', scores, valueset[number].astype(jnp.float32),...  19.7 us
    dot_general x6, matrix products, shards(): jnp.einsum('ihd,hde->ihe', queries[number].astype(jnp.float32), carried,...  13.2 us
    reshape x2, local copies, waits for them, and re-layouts, shards(): keyset = key_rows.reshape(block_count, BLOCK, head_count, HD)  11.5 us
  transfers between devices with their start and end apart: 1, of which 0 were waited for; matrix products, arithmetic and copies ran while one was open for 21% of the time, Pallas kernels for 0%

commit v1 on v0

v1 whole, which is shorter than its diff:
```python
import functools

import jax
import jax.numpy as jnp
from jax import lax
from jax.experimental import pallas as pl
from jax.experimental.pallas import tpu as pltpu
from jax.sharding import PartitionSpec as P

HEADS = 32
HD = 128
CHUNK = 128
GROUP = 1024
PIECE = 16
NZ, NX = 8, 4
SPLIT = 12
MESH = pl.DeviceIdType.MESH


def offsets():
    def hops(offset):
        return min(offset[0], NZ - offset[0]) + min(offset[1], NX - offset[1])

    pairs = [(dz, dx) for dz in range(NZ) for dx in range(NX) if dz or dx]
    return sorted(pairs, key=hops, reverse=True)


def send(src, dst, send_sem, recv_sem, device):
    pltpu.make_async_remote_copy(
        src_ref=src,
        dst_ref=dst,
        send_sem=send_sem,
        recv_sem=recv_sem,
        device_id=device,
        device_id_type=MESH,
    ).start()


def wait_bytes(ref, sem):
    pltpu.make_async_copy(ref, ref, sem).wait()


def halves(x):
    high = x.astype(jnp.bfloat16)
    return high, (x - high.astype(jnp.float32)).astype(jnp.bfloat16)


def kernel(
    starts,
    q_hbm,
    k_hbm,
    v_hbm,
    gain_ref,
    out_hbm,
    q_ref,
    k_ref,
    v_ref,
    att,
    out_ref,
    state,
    summ,
    gath,
    sums,
    incoming,
    squares,
    squares_in,
    load_sem,
    store_sem,
    ctx_send,
    ctx_recv,
    head_send,
    head_recv,
):
    rows = q_ref.shape[0]
    head_count = q_ref.shape[1] // HD
    groups = rows // GROUP
    blocks = GROUP // 128
    docs = starts.shape[0]
    peers = NZ * NX
    teams = lax.axis_size("head")

    loads = []
    for g in range(groups):
        part = pl.ds(g * GROUP, GROUP)
        loads.append(pltpu.make_async_copy(k_hbm.at[part], k_ref.at[part], load_sem.at[0, g]))
        loads.append(pltpu.make_async_copy(v_hbm.at[part], v_ref.at[part], load_sem.at[1, g]))
    for g in range(groups):
        part = pl.ds(g * GROUP, GROUP)
        loads.append(pltpu.make_async_copy(q_hbm.at[part], q_ref.at[part], load_sem.at[2, g]))
    for load in loads:
        load.start()

    me = lax.axis_index("ctx")
    team = lax.axis_index("head")
    z, x = me // NX, me % NX
    owners = [lax.rem(z + dz, NZ) * NX + lax.rem(x + dx, NX) for dz, dx in offsets()]
    mates = [lax.rem(team + d, teams) for d in (4, 5, 3, 2, 6, 1, 7)]
    barrier = pltpu.get_barrier_semaphore()
    for t in owners:
        pl.semaphore_signal(barrier, inc=1, device_id={"ctx": t}, device_id_type=MESH)
    for t in mates:
        pl.semaphore_signal(barrier, inc=1, device_id={"head": t}, device_id_type=MESH)

    anchor = me * rows
    start = [starts[d] for d in range(docs)]

    def last_start(position):
        last = start[0]
        for d in range(1, docs):
            last = jnp.where(start[d] <= position, start[d], last)
        return last

    def first_start(position):
        first = jnp.int32(2**30)
        for d in range(docs - 1, -1, -1):
            first = jnp.where(start[d] >= position, start[d], first)
        return first

    tail = last_start(anchor + rows - 1) - anchor
    row = lax.broadcasted_iota(jnp.int32, (GROUP, HD), 0)
    for g in range(groups):
        loads[2 * g].wait()
        loads[2 * g + 1].wait()
        part = pl.ds(g * GROUP, GROUP)
        keep = jnp.where(row + g * GROUP >= tail, 1.0, 0.0).astype(jnp.bfloat16)
        for h in range(head_count):
            lanes = pl.ds(h * HD, HD)
            add = lax.dot_general(
                k_ref[part, lanes] * keep,
                v_ref[part, lanes],
                (((0,), (0,)), ((), ())),
                preferred_element_type=jnp.float32,
            ).reshape(NZ, PIECE, HD)
            summ[:, h] = add if g == 0 else summ[:, h] + add

    pl.semaphore_wait(barrier, peers - 1 + teams - 1)
    for (dz, dx), t in zip(offsets(), owners):
        tz, tx = lax.rem(z + dz, NZ), lax.rem(x + dx, NX)
        send(summ.at[tz, tx], gath.at[me], ctx_send.at[0], ctx_recv.at[0], {"ctx": t})
    gath[me] = summ[z, x]

    for g in range(groups):
        loads[2 * groups + g].wait()
    state[...] = jnp.zeros_like(state)

    def local(c, _):
        r0 = pl.multiple_of(c * CHUNK, CHUNK)
        part = pl.ds(r0, CHUNK)
        base = anchor + r0
        position = base + lax.broadcasted_iota(jnp.int32, (CHUNK, HD), 0)
        source = base + lax.broadcasted_iota(jnp.int32, (CHUNK, CHUNK), 1)
        since = jnp.full((CHUNK, HD), start[0], jnp.int32)
        for d in range(1, docs):
            since = jnp.where(position >= start[d], start[d], since)
        allowed = (source <= position) & (source >= since)
        final = last_start(base + CHUNK - 1)
        live = jnp.where(position < first_start(base), 1.0, 0.0).astype(jnp.bfloat16)
        keep = jnp.where(position >= final, 1.0, 0.0).astype(jnp.bfloat16)
        carry_on = jnp.where(final >= base, 0.0, 1.0)
        for h in range(head_count):
            lanes = pl.ds(h * HD, HD)
            q, k, v = q_ref[part, lanes], k_ref[part, lanes], v_ref[part, lanes]
            scores = lax.dot_general(
                q, k, (((1,), (1,)), ((), ())), preferred_element_type=jnp.float32
            )
            s_high, s_low = halves(jnp.where(allowed, scores, 0.0))
            before = state[h]
            b_high, b_low = halves(before)
            q_live = q * live
            within = jnp.dot(
                jnp.concatenate([s_high, s_low], axis=1),
                jnp.concatenate([v, v], axis=0),
                preferred_element_type=jnp.float32,
            )
            across = jnp.dot(
                jnp.concatenate([q_live, q_live], axis=1),
                jnp.concatenate([b_high, b_low], axis=0),
                preferred_element_type=jnp.float32,
            )
            att[part, lanes] = within + across
            contrib = lax.dot_general(
                k * keep, v, (((0,), (0,)), ((), ())), preferred_element_type=jnp.float32
            )
            state[h] = before * carry_on + contrib
        return 0

    lax.fori_loop(0, SPLIT, local, 0)

    slab = lax.broadcasted_iota(jnp.int32, (peers, HD), 0)
    since = jnp.full((peers, HD), start[0], jnp.int32)
    for d in range(1, docs):
        since = jnp.where((slab + 1) * rows - 1 >= start[d], start[d], since)
    going_on = jnp.where(since >= slab * rows, 0.0, 1.0)
    wait_bytes(gath.at[pl.ds(0, peers - 1)], ctx_recv.at[0])
    carry = jnp.zeros((PIECE, HD), jnp.float32)
    for m in range(peers):
        sums[m] = carry
        carry = carry * going_on[m : m + 1] + gath[m]
    for t in owners:
        send(sums.at[t], incoming.at[me], ctx_send.at[1], ctx_recv.at[1], {"ctx": t})
    incoming[me] = sums[me]

    lax.fori_loop(SPLIT, rows // CHUNK, local, 0)

    wait_bytes(incoming.at[pl.ds(0, peers - 1)], ctx_recv.at[1])
    entry = first_start(anchor) - anchor
    entering = []
    for h in range(head_count):
        whole = jnp.concatenate([incoming[s * NX + h] for s in range(NZ)], axis=0)
        entering.append(jnp.concatenate(halves(whole), axis=0))
    eye = lax.broadcasted_iota(jnp.int32, (128, 128), 0) == lax.broadcasted_iota(
        jnp.int32, (128, 128), 1
    )
    for g in range(groups):

        def finish(b, _, g=g):
            r0 = pl.multiple_of(g * GROUP + b * 128, 128)
            part = pl.ds(r0, 128)
            position = r0 + lax.broadcasted_iota(jnp.int32, (128, HD), 0)
            live = jnp.where(position < entry, 1.0, 0.0).astype(jnp.bfloat16)
            total = jnp.zeros((128, HD), jnp.float32)
            for h in range(head_count):
                lanes = pl.ds(h * HD, HD)
                q = q_ref[part, lanes] * live
                a = att[part, lanes] + jnp.dot(
                    jnp.concatenate([q, q], axis=1),
                    entering[h],
                    preferred_element_type=jnp.float32,
                )
                att[part, lanes] = a
                total = total + a * a
            column = jnp.sum(total, axis=1, keepdims=True)
            squares[g, pl.ds(b, 1)] = jnp.sum(
                jnp.where(eye, column, 0.0), axis=0, keepdims=True
            )
            return 0

        lax.fori_loop(0, blocks, finish, 0)
        for t in mates:
            send(
                squares.at[g], squares_in.at[g, team], head_send.at[g], head_recv.at[g], {"head": t}
            )
        squares_in[g, team] = squares[g]

    gain = gain_ref[...].astype(jnp.float32)
    stores = []
    for g in range(groups):
        wait_bytes(squares_in.at[g, pl.ds(0, teams - 1)], head_recv.at[g])
        total = squares_in[g, 0]
        for m in range(1, teams):
            total = total + squares_in[g, m]
        scale = lax.rsqrt(total / (HEADS * HD) + 1e-06)
        for b in range(blocks):
            part = pl.ds(g * GROUP + b * 128, 128)
            column = jnp.sum(jnp.where(eye, scale[b : b + 1], 0.0), axis=1, keepdims=True)
            out_ref[part] = (att[part] * column * gain).astype(jnp.bfloat16)
        part = pl.ds(g * GROUP, GROUP)
        store = pltpu.make_async_copy(out_ref.at[part], out_hbm.at[part], store_sem.at[g])
        store.start()
        stores.append(store)

    for store in stores:
        store.wait()
    for side in range(2):
        wait_bytes((gath, incoming)[side].at[pl.ds(0, peers - 1)], ctx_send.at[side])
    for g in range(groups):
        wait_bytes(squares_in.at[g, pl.ds(0, teams - 1)], head_send.at[g])


def shards(query_rows, key_rows, value_rows, out_gain, doc_starts):
    rows, features = query_rows.shape
    head_count = features // HD
    groups = rows // GROUP
    peers = lax.axis_size("ctx")
    teams = lax.axis_size("head")
    smem = pl.BlockSpec(memory_space=pltpu.SMEM)
    hbm = pl.BlockSpec(memory_space=pl.ANY)
    vmem = pl.BlockSpec(memory_space=pltpu.VMEM)
    f32 = jnp.float32
    dma = pltpu.SemaphoreType.DMA
    return pl.pallas_call(
        kernel,
        out_shape=jax.ShapeDtypeStruct((rows, features), jnp.bfloat16),
        in_specs=[smem, hbm, hbm, hbm, vmem],
        out_specs=hbm,
        scratch_shapes=[
            pltpu.VMEM((rows, features), jnp.bfloat16),
            pltpu.VMEM((rows, features), jnp.bfloat16),
            pltpu.VMEM((rows, features), jnp.bfloat16),
            pltpu.VMEM((rows, features), f32),
            pltpu.VMEM((rows, features), jnp.bfloat16),
            pltpu.VMEM((head_count, HD, HD), f32),
            pltpu.VMEM((NZ, NX, PIECE, HD), f32),
            pltpu.VMEM((peers, PIECE, HD), f32),
            pltpu.VMEM((peers, PIECE, HD), f32),
            pltpu.VMEM((peers, PIECE, HD), f32),
            pltpu.VMEM((groups, GROUP // 128, 128), f32),
            pltpu.VMEM((groups, teams, GROUP // 128, 128), f32),
            dma((3, groups)),
            dma((groups,)),
            dma((2,)),
            dma((2,)),
            dma((groups,)),
            dma((groups,)),
        ],
        compiler_params=pltpu.CompilerParams(
            collective_id=0, has_side_effects=True, vmem_limit_bytes=48 * 2**20
        ),
    )(doc_starts, query_rows, key_rows, value_rows, out_gain.reshape(1, features))


def solution(mesh):
    placed = (P("ctx", "head"), P("ctx", "head"), P("ctx", "head"), P("head"), P())
    return jax.shard_map(
        shards, mesh=mesh, in_specs=placed, out_specs=P("ctx", "head"), check_vma=False
    )
```

time: 319 us -> 46.3 us (0.15)
  blocking collectives: 101 us -> 0 us
  other arithmetic: 95.8 us -> 0 us
  local copies, waits for them, and re-layouts: 62.4 us -> 3 us
  Pallas kernels: 0 us -> 43.2 us
  matrix products: 42.3 us -> 0 us
  between operations: 13.9 us -> 0.01 us
    unnamed x1 -> x0, blocking collectives: 66.2 us -> none
    select_n x34 -> x0, other arithmetic: 61.6 us -> none  [the longest x32 54.6 us: hop(): return jax.tree.map(lambda a, b: jnp.where(reached, a, b), new, before)]
    pallas_call x0 -> x1, Pallas kernels: none -> 43.2 us  [shards(): pl.pallas_call(kernel, out_shape=jax.ShapeDtypeStruct((rows, features), j...]
    dot_general x19 -> x0, matrix products: 42.3 us -> none  [the longest x6 19.7 us: shards(): jnp.einsum('hij,jhe->ihe', scores, valueset[number].astype(jnp.float32),...]
    psum x1 -> x0, blocking collectives: 35 us -> none  [shards(): totals = lax.psum(local_squares, 'head')]
    unnamed x93 -> x3, local copies, waits for them, and re-layouts: 28.2 us -> 2.32 us
    gt x32 -> x0, other arithmetic: 19.7 us -> none  [combine(): joined = jnp.where(later[1][0] > 0.0, later[0], earlier[0] + later[0])]
    reshape x3 -> x1, local copies, waits for them, and re-layouts: 14.5 us -> 0.68 us  [shards(): out_gain.reshape(1, features)]
  transfers between devices with their start and end apart: 1 -> 0, of which waited for: 0 -> 0; matrix products, arithmetic and copies ran while one was open for 21% -> 0% of each run, Pallas kernels for 0% -> 0%
where the time goes in v1:
time: 46.3 us; the launch traced here: 46.2 us
  Pallas kernels  43.2 us (93%)
  local copies, waits for them, and re-layouts  3 us (6%)
    pallas_call x1, Pallas kernels, shards(): pl.pallas_call(kernel, out_shape=jax.ShapeDtypeStruct((rows, features), j...  43.2 us
    unnamed x3, local copies, waits for them, and re-layouts  2.32 us

profile of v1, /device:TPU:1, one launch (start us, length us, event | category | flops | bytes accessed | tf_op | source)
XLA Modules:
  0.0 46.2 jit_solution(9700062286108977705)
XLA Ops:
  0.0 0.7 %reshape.3.gain_ref = bf16[1,512]{1,0:T(2,128)(2,1)S(1)} reshape(bf16[512]{0:T(512)(128)(2,1)} %param.8) | data formatting | bytes 2048 | tf_op jit(solution)/shard_map/reshape | solution.py:309
  0.7 0.0 copy-start
  0.7 0.7 %copy-done = s32[16]{0:T(128)S(1)} copy-done((s32[16]{0:T(128)S(1)}, s32[16]{0:T(128)}, u32[]{:S(2)}) %copy-start) | copy-done | bytes 88
  1.3 43.2 %shard_map.55 = bf16[3072,512]{1,0:T(8,128)(2,1)S(1)} custom-call(s32[16]{0:T(128)S(1)} %copy-done, bf16[3072,512]{1,0:T(8,128)(2,1)} %q_hbm.1, bf16[3072,512]{1,0:T(8,128)(2,1)} %k_hbm.1, bf16[3072,512]{1,0:T(8,128)(2,1)} %v_hbm.1, bf16[1,512]{1,0:T(2,128)(2,1)S(1)} %reshape.3.gain_ref), custom_call_target="tpu_custom_call" | custom-call | tf_op jit(solution)/shard_map/pallas_call | solution.py:281
  44.6 1.7 %copy.7 = bf16[3072,512]{1,0:T(8,128)(2,1)} copy(bf16[3072,512]{1,0:T(8,128)(2,1)S(1)} %shard_map.55) | data formatting | bytes 6291456
Async XLA Ops:
  0.7 0.7 %copy-start = (s32[16]{0:T(128)S(1)}, s32[16]{0:T(128)}, u32[]{:S(2)}) copy-start(s32[16]{0:T(128)} %starts.1) | copy-start | bytes 196

commit v2 on v1

--- a/solution.py
+++ b/solution.py
@@ -14,6 +14,7 @@
 PIECE = 16
 NZ, NX = 8, 4
 SPLIT = 12
+FINAL = 512
 MESH = pl.DeviceIdType.MESH
 
 
@@ -45,18 +46,34 @@
     return high, (x - high.astype(jnp.float32)).astype(jnp.bfloat16)
 
 
+def diagonal(first, second):
+    zeros = jnp.zeros_like(first)
+    return jnp.concatenate(
+        [jnp.concatenate([first, zeros], axis=1), jnp.concatenate([zeros, second], axis=1)], axis=0
+    )
+
+
+def apart(pair):
+    return diagonal(pair[:, :HD], pair[:, HD:])
+
+
+def dot(a, b):
+    return jnp.dot(a, b, preferred_element_type=jnp.float32)
+
+
 def kernel(
-    starts,
+    starts_hbm,
     q_hbm,
     k_hbm,
     v_hbm,
+    gain_hbm,
+    out_ref,
+    starts,
     gain_ref,
-    out_hbm,
     q_ref,
     k_ref,
     v_ref,
     att,
-    out_ref,
     state,
     summ,
     gath,
@@ -65,7 +82,7 @@
     squares,
     squares_in,
     load_sem,
-    store_sem,
+    small_sem,
     ctx_send,
     ctx_recv,
     head_send,
@@ -79,17 +96,6 @@
     peers = NZ * NX
     teams = lax.axis_size("head")
 
-    loads = []
-    for g in range(groups):
-        part = pl.ds(g * GROUP, GROUP)
-        loads.append(pltpu.make_async_copy(k_hbm.at[part], k_ref.at[part], load_sem.at[0, g]))
-        loads.append(pltpu.make_async_copy(v_hbm.at[part], v_ref.at[part], load_sem.at[1, g]))
-    for g in range(groups):
-        part = pl.ds(g * GROUP, GROUP)
-        loads.append(pltpu.make_async_copy(q_hbm.at[part], q_ref.at[part], load_sem.at[2, g]))
-    for load in loads:
-        load.start()
-
     me = lax.axis_index("ctx")
     team = lax.axis_index("head")
     z, x = me // NX, me % NX
@@ -101,6 +107,23 @@
     for t in mates:
         pl.semaphore_signal(barrier, inc=1, device_id={"head": t}, device_id_type=MESH)
 
+    small = [
+        pltpu.make_async_copy(starts_hbm, starts, small_sem.at[0]),
+        pltpu.make_async_copy(gain_hbm, gain_ref, small_sem.at[1]),
+    ]
+    loads = []
+    for g in range(groups):
+        part = pl.ds(g * GROUP, GROUP)
+        loads.append(pltpu.make_async_copy(k_hbm.at[part], k_ref.at[part], load_sem.at[0, g]))
+        loads.append(pltpu.make_async_copy(v_hbm.at[part], v_ref.at[part], load_sem.at[1, g]))
+    for g in range(groups):
+        part = pl.ds(g * GROUP, GROUP)
+        loads.append(pltpu.make_async_copy(q_hbm.at[part], q_ref.at[part], load_sem.at[2, g]))
+    for load in small + loads:
+        load.start()
+
+    small[0].wait()
+    small[1].wait()
     anchor = me * rows
     start = [starts[d] for d in range(docs)]
 
@@ -152,36 +175,33 @@
         since = jnp.full((CHUNK, HD), start[0], jnp.int32)
         for d in range(1, docs):
             since = jnp.where(position >= start[d], start[d], since)
-        allowed = (source <= position) & (source >= since)
+        allowed = jnp.where((source <= position) & (source >= since), 1.0, 0.0)
+        allowed = jnp.concatenate([allowed, allowed], axis=1) > 0.0
         final = last_start(base + CHUNK - 1)
         live = jnp.where(position < first_start(base), 1.0, 0.0).astype(jnp.bfloat16)
+        live = jnp.concatenate([live, live], axis=1)
         keep = jnp.where(position >= final, 1.0, 0.0).astype(jnp.bfloat16)
+        keep = jnp.concatenate([keep, keep], axis=1)
         carry_on = jnp.where(final >= base, 0.0, 1.0)
-        for h in range(head_count):
-            lanes = pl.ds(h * HD, HD)
+        for p in range(head_count // 2):
+            lanes = pl.ds(p * 2 * HD, 2 * HD)
             q, k, v = q_ref[part, lanes], k_ref[part, lanes], v_ref[part, lanes]
             scores = lax.dot_general(
-                q, k, (((1,), (1,)), ((), ())), preferred_element_type=jnp.float32
+                q, apart(k), (((1,), (1,)), ((), ())), preferred_element_type=jnp.float32
             )
             s_high, s_low = halves(jnp.where(allowed, scores, 0.0))
-            before = state[h]
+            before = state[p]
             b_high, b_low = halves(before)
+            kept = k * keep
+            turned = jnp.concatenate([kept[:, :HD].T, kept[:, HD:].T], axis=1)
+            inner = dot(jnp.concatenate([s_high, s_low, turned], axis=0), apart(v))
             q_live = q * live
-            within = jnp.dot(
-                jnp.concatenate([s_high, s_low], axis=1),
-                jnp.concatenate([v, v], axis=0),
-                preferred_element_type=jnp.float32,
+            across = dot(
+                jnp.concatenate([q_live, q_live], axis=1),
+                jnp.concatenate([apart(b_high), apart(b_low)], axis=0),
             )
-            across = jnp.dot(
-                jnp.concatenate([q_live, q_live], axis=1),
-                jnp.concatenate([b_high, b_low], axis=0),
-                preferred_element_type=jnp.float32,
-            )
-            att[part, lanes] = within + across
-            contrib = lax.dot_general(
-                k * keep, v, (((0,), (0,)), ((), ())), preferred_element_type=jnp.float32
-            )
-            state[h] = before * carry_on + contrib
+            att[part, lanes] = inner[:CHUNK] + inner[CHUNK : 2 * CHUNK] + across
+            state[p] = before * carry_on + inner[2 * CHUNK :]
         return 0
 
     lax.fori_loop(0, SPLIT, local, 0)
@@ -205,45 +225,46 @@
     wait_bytes(incoming.at[pl.ds(0, peers - 1)], ctx_recv.at[1])
     entry = first_start(anchor) - anchor
     entering = []
-    for h in range(head_count):
-        whole = jnp.concatenate([incoming[s * NX + h] for s in range(NZ)], axis=0)
-        entering.append(jnp.concatenate(halves(whole), axis=0))
+    for p in range(head_count // 2):
+        heads = []
+        for h in (2 * p, 2 * p + 1):
+            heads.append(jnp.concatenate([incoming[s * NX + h] for s in range(NZ)], axis=0))
+        high, low = halves(jnp.concatenate(heads, axis=1))
+        entering.append(jnp.concatenate([apart(high), apart(low)], axis=0))
     eye = lax.broadcasted_iota(jnp.int32, (128, 128), 0) == lax.broadcasted_iota(
         jnp.int32, (128, 128), 1
     )
     for g in range(groups):
 
         def finish(b, _, g=g):
-            r0 = pl.multiple_of(g * GROUP + b * 128, 128)
-            part = pl.ds(r0, 128)
-            position = r0 + lax.broadcasted_iota(jnp.int32, (128, HD), 0)
+            r0 = pl.multiple_of(g * GROUP + b * FINAL, FINAL)
+            part = pl.ds(r0, FINAL)
+            position = r0 + lax.broadcasted_iota(jnp.int32, (FINAL, HD), 0)
             live = jnp.where(position < entry, 1.0, 0.0).astype(jnp.bfloat16)
-            total = jnp.zeros((128, HD), jnp.float32)
-            for h in range(head_count):
-                lanes = pl.ds(h * HD, HD)
+            live = jnp.concatenate([live, live], axis=1)
+            total = jnp.zeros((FINAL, 2 * HD), jnp.float32)
+            for p in range(head_count // 2):
+                lanes = pl.ds(p * 2 * HD, 2 * HD)
                 q = q_ref[part, lanes] * live
-                a = att[part, lanes] + jnp.dot(
-                    jnp.concatenate([q, q], axis=1),
-                    entering[h],
-                    preferred_element_type=jnp.float32,
-                )
+                a = att[part, lanes] + dot(jnp.concatenate([q, q], axis=1), entering[p])
                 att[part, lanes] = a
                 total = total + a * a
+            total = total[:, :HD] + total[:, HD:]
             column = jnp.sum(total, axis=1, keepdims=True)
-            squares[g, pl.ds(b, 1)] = jnp.sum(
-                jnp.where(eye, column, 0.0), axis=0, keepdims=True
-            )
+            for i in range(FINAL // 128):
+                squares[g, pl.ds(b * (FINAL // 128) + i, 1)] = jnp.sum(
+                    jnp.where(eye, column[i * 128 : i * 128 + 128], 0.0), axis=0, keepdims=True
+                )
             return 0
 
-        lax.fori_loop(0, blocks, finish, 0)
+        lax.fori_loop(0, GROUP // FINAL, finish, 0)
         for t in mates:
             send(
                 squares.at[g], squares_in.at[g, team], head_send.at[g], head_recv.at[g], {"head": t}
             )
         squares_in[g, team] = squares[g]
 
-    gain = gain_ref[...].astype(jnp.float32)
-    stores = []
+    gain = gain_ref[...].astype(jnp.float32).reshape(1, head_count * HD)
     for g in range(groups):
         wait_bytes(squares_in.at[g, pl.ds(0, teams - 1)], head_recv.at[g])
         total = squares_in[g, 0]
@@ -254,13 +275,7 @@
             part = pl.ds(g * GROUP + b * 128, 128)
             column = jnp.sum(jnp.where(eye, scale[b : b + 1], 0.0), axis=1, keepdims=True)
             out_ref[part] = (att[part] * column * gain).astype(jnp.bfloat16)
-        part = pl.ds(g * GROUP, GROUP)
-        store = pltpu.make_async_copy(out_ref.at[part], out_hbm.at[part], store_sem.at[g])
-        store.start()
-        stores.append(store)
-
-    for store in stores:
-        store.wait()
+
     for side in range(2):
         wait_bytes((gath, incoming)[side].at[pl.ds(0, peers - 1)], ctx_send.at[side])
     for g in range(groups):
@@ -273,23 +288,27 @@
     groups = rows // GROUP
     peers = lax.axis_size("ctx")
     teams = lax.axis_size("head")
-    smem = pl.BlockSpec(memory_space=pltpu.SMEM)
-    hbm = pl.BlockSpec(memory_space=pl.ANY)
+    hbm = pl.BlockSpec(memory_space=pltpu.HBM)
     vmem = pl.BlockSpec(memory_space=pltpu.VMEM)
     f32 = jnp.float32
     dma = pltpu.SemaphoreType.DMA
+    operands = [
+        pltpu.with_memory_space_constraint(array, pltpu.HBM)
+        for array in (doc_starts, query_rows, key_rows, value_rows, out_gain)
+    ]
     return pl.pallas_call(
         kernel,
         out_shape=jax.ShapeDtypeStruct((rows, features), jnp.bfloat16),
-        in_specs=[smem, hbm, hbm, hbm, vmem],
-        out_specs=hbm,
+        in_specs=[hbm] * 5,
+        out_specs=vmem,
         scratch_shapes=[
+            pltpu.SMEM(doc_starts.shape, jnp.int32),
+            pltpu.VMEM(out_gain.shape, jnp.bfloat16),
             pltpu.VMEM((rows, features), jnp.bfloat16),
             pltpu.VMEM((rows, features), jnp.bfloat16),
             pltpu.VMEM((rows, features), jnp.bfloat16),
             pltpu.VMEM((rows, features), f32),
-            pltpu.VMEM((rows, features), jnp.bfloat16),
-            pltpu.VMEM((head_count, HD, HD), f32),
+            pltpu.VMEM((head_count // 2, HD, 2 * HD), f32),
             pltpu.VMEM((NZ, NX, PIECE, HD), f32),
             pltpu.VMEM((peers, PIECE, HD), f32),
             pltpu.VMEM((peers, PIECE, HD), f32),
@@ -297,7 +316,7 @@
             pltpu.VMEM((groups, GROUP // 128, 128), f32),
             pltpu.VMEM((groups, teams, GROUP // 128, 128), f32),
             dma((3, groups)),
-            dma((groups,)),
+            dma((2,)),
             dma((2,)),
             dma((2,)),
             dma((groups,)),
@@ -306,7 +325,7 @@
         compiler_params=pltpu.CompilerParams(
             collective_id=0, has_side_effects=True, vmem_limit_bytes=48 * 2**20
         ),
-    )(doc_starts, query_rows, key_rows, value_rows, out_gain.reshape(1, features))
+    )(*operands)
 
 
 def solution(mesh):

time: 46.3 us -> 37.8 us (0.82)
  Pallas kernels: 43.2 us -> 36.1 us
  local copies, waits for them, and re-layouts: 3 us -> 1.67 us
    pallas_call x1, Pallas kernels: 43.2 us -> 36.1 us  [shards(): pl.pallas_call(kernel, out_shape=jax.ShapeDtypeStruct((rows, features), j...]
    reshape x1 -> x0, local copies, waits for them, and re-layouts: 0.68 us -> none  [shards(): out_gain.reshape(1, features)]
    unnamed x3 -> x1, local copies, waits for them, and re-layouts: 2.32 us -> 1.67 us
where the time goes in v2:
time: 37.8 us; the launch traced here: 37.7 us
  Pallas kernels  36.1 us (96%)
  local copies, waits for them, and re-layouts  1.67 us (4%)
    pallas_call x1, Pallas kernels, shards(): pl.pallas_call(kernel, out_shape=jax.ShapeDtypeStruct((rows, features), j...  36.1 us
    unnamed x1, local copies, waits for them, and re-layouts  1.67 us

profile of v2, /device:TPU:1, one launch (start us, length us, event | category | flops | bytes accessed | tf_op | source)
XLA Modules:
  0.0 37.7 jit_solution(5564326073699374601)
XLA Ops:
  0.0 36.1 %shard_map.55 = bf16[3072,512]{1,0:T(8,128)(2,1)S(1)} custom-call(s32[16]{0:T(128)} %starts_hbm.1, bf16[3072,512]{1,0:T(8,128)(2,1)} %q_hbm.1, bf16[3072,512]{1,0:T(8,128)(2,1)} %k_hbm.1, bf16[3072,512]{1,0:T(8,128)(2,1)} %v_hbm.1, bf16[512]{0:T(512)(128)(2,1)} %gain_hbm.1), custom_call_target="tpu_custom_call" | custom-call | tf_op jit(solution)/shard_map/pallas_call | solution.py:299
  36.1 1.7 %copy.7 = bf16[3072,512]{1,0:T(8,128)(2,1)} copy(bf16[3072,512]{1,0:T(8,128)(2,1)S(1)} %shard_map.55) | data formatting | bytes 6291456
